TPU v7x, 32 devices: a whole 2x2x4 slice. The times are simulated.
32 devices in a mesh: dp: 4 (over y, core), ctx: 8 (over z, x).
Axes of the slice: x: 2, y: 2, z: 4, core: 2. Of those that a mesh axis runs over, the one named last changes fastest.
Arguments:
- queries: bfloat16 [4096, 2048], P(('dp', 'ctx')), may hold values from -6 to 6
- key_rows: bfloat16 [4096, 2048], P(('dp', 'ctx')), may hold values from -6 to 6
- value_rows: bfloat16 [4096, 2048], P(('dp', 'ctx')), may hold values from -6 to 6
- hidden_in: bfloat16 [4096, 2304], P(('dp', 'ctx')), may hold values from -6 to 6
- beta_weight: bfloat16 [2304, 16], replicated, may hold values from -0.125 to 0.125
- log_gate: float32 [16, 4096], P(None, ('dp', 'ctx')), may hold values from -1 to 0
- out_grad: bfloat16 [4096, 2048], P(('dp', 'ctx')), may hold values from -24 to 24
- lengths: int32 [4, 4], P('dp'), may hold values from 1 to 512, 1024 in all within a row
- rewards: float32 [16], replicated, may hold values from -6 to 6
- prompts: int32 [16], replicated, may hold values from 0 to 3
Outputs:
- query_grad: bfloat16 [4096, 2048], P(('dp', 'ctx'))
- key_grad: bfloat16 [4096, 2048], P(('dp', 'ctx'))
- value_grad: bfloat16 [4096, 2048], P(('dp', 'ctx'))
- gate_grad: float32 [16, 4096], P(None, ('dp', 'ctx'))
- beta_weight_grad: float32 [2304, 16], P(('dp', 'ctx'))
Inputs may be any that keep to these rules, and one draw needn't show every extreme that they name: `lengths`: each row sums to 1024; its largest entry is exactly 512.
All inputs are finite; a program needn't handle non-finite values.
Results may differ from a plain program's by a relative error of at most 0.001.
Values sent between devices are 32-bit elements; how exact they have to be, the bound alone decides.
A program may use at most 128 MiB of HBM per device.

v0:
```python
import jax
import jax.numpy as jnp
from jax import lax
from jax.sharding import PartitionSpec as P

BLOCK = 64


highest = lax.Precision.HIGHEST


def from_behind(x, axis, by):
    length = lax.axis_size(axis)
    pairs = [(i, i + by) for i in range(length) if 0 <= i + by < length]
    return lax.ppermute(x, axis, pairs)


def unit_rows(rows):
    return rows * lax.rsqrt(jnp.sum(rows * rows, axis=-1, keepdims=True) + 1e-06)


def unit_inverse(lower_part):
    size = lower_part.shape[-1]
    nilpotent = -lower_part
    total = jnp.eye(size, dtype=jnp.float32) + nilpotent
    power = nilpotent
    for level in range(max(1, (size - 1).bit_length()) - 1):
        power = jnp.einsum("nhij,nhjk->nhik", power, power, precision=highest)
        total = total + jnp.einsum("nhij,nhjk->nhik", total, power, precision=highest)
    return total


def block_terms(queries, key_rows, value_rows, beta, gate_log, starts):
    size = queries.shape[2]
    row_ids = lax.broadcasted_iota(jnp.int32, (size, size), 0)
    col_ids = lax.broadcasted_iota(jnp.int32, (size, size), 1)
    gamma = jnp.cumsum(gate_log, axis=-1)
    count = jnp.cumsum(starts, axis=-1)
    linked = (count[:, :, None] == count[:, None, :]) & (row_ids >= col_ids)
    linked = linked[:, None, :, :]
    spread = gamma[..., :, None] - gamma[..., None, :]
    decay = jnp.where(linked, jnp.exp(jnp.where(linked, spread, 0.0)), 0.0)
    head_decay = jnp.where(count == 0.0, 1.0, 0.0)[:, None, :] * jnp.exp(gamma)
    tail_decay = decay[..., size - 1, :]
    key_key = jnp.einsum("nhik,nhjk->nhij", key_rows, key_rows, precision=highest)
    lower_part = jnp.where(row_ids > col_ids, beta[..., :, None] * decay * key_key, 0.0)
    inverse = unit_inverse(lower_part)
    rhs_value = beta[..., None] * value_rows
    rhs_key = (beta * head_decay)[..., None] * key_rows
    u_zero = jnp.einsum("nhij,nhjv->nhiv", inverse, rhs_value, precision=highest)
    z_rows = jnp.einsum("nhij,nhjk->nhik", inverse, rhs_key, precision=highest)
    mixing = decay * jnp.einsum("nhik,nhjk->nhij", queries, key_rows, precision=highest)
    out_zero = jnp.einsum("nhij,nhjv->nhiv", mixing, u_zero, precision=highest)
    carry_q = head_decay[..., None] * queries - jnp.einsum(
        "nhij,nhjk->nhik", mixing, z_rows, precision=highest
    )
    weighted = tail_decay[..., None] * key_rows
    state_zero = jnp.einsum("nhcv,nhck->nhvk", u_zero, weighted, precision=highest)
    identity = jnp.eye(key_rows.shape[-1], dtype=jnp.float32)
    transfer = head_decay[..., size - 1][..., None, None] * identity - jnp.einsum(
        "nhck,nhcj->nhkj", z_rows, weighted, precision=highest
    )
    return (out_zero, carry_q, state_zero, transfer)


def run_blocks(out_zero, carry_q, state_zero, transfer, state_in):

    def advance(state, pieces):
        piece_out, piece_q, piece_state, piece_map = pieces
        result = piece_out + jnp.einsum("hck,hvk->hcv", piece_q, state, precision=highest)
        updated = jnp.einsum("hvk,hkj->hvj", state, piece_map, precision=highest) + piece_state
        return (updated, result)

    final, outputs = lax.scan(advance, state_in, (out_zero, carry_q, state_zero, transfer))
    return (outputs, final)


def segment_terms(query_f, key_f, value_f, logits, gate_log, starts):
    token_count, heads = logits.shape
    blocks = token_count // BLOCK

    def split(rows):
        return rows.reshape(blocks, BLOCK, heads, -1).transpose(0, 2, 1, 3)

    beta = jax.nn.sigmoid(logits).reshape(blocks, BLOCK, heads).transpose(0, 2, 1)
    gates = gate_log.reshape(heads, blocks, BLOCK).transpose(1, 0, 2)
    return block_terms(
        unit_rows(split(query_f)),
        unit_rows(split(key_f)),
        split(value_f),
        beta,
        gates,
        starts.reshape(blocks, BLOCK),
    )


def output_from_terms(terms, state_in):
    outputs, final = run_blocks(terms[0], terms[1], terms[2], terms[3], state_in)
    token_count = outputs.shape[0] * outputs.shape[2]
    return (outputs.transpose(0, 2, 1, 3).reshape(token_count, -1), final)


def segment_map(terms, zero_state):

    def compose_step(carry, pieces):
        linear, offset = carry
        piece_state, piece_map = pieces
        linear = jnp.einsum("hij,hjk->hik", linear, piece_map, precision=highest)
        offset = jnp.einsum("hvk,hkj->hvj", offset, piece_map, precision=highest) + piece_state
        return ((linear, offset), None)

    start_map = jnp.broadcast_to(jnp.eye(zero_state.shape[-1], dtype=jnp.float32), zero_state.shape)
    result, unused = lax.scan(compose_step, (start_map, zero_state), (terms[2], terms[3]))
    return result


def token_plan(row_lengths, positions):
    ends = jnp.cumsum(row_lengths)
    begins = ends - row_lengths
    starts = jnp.any(positions[:, None] == begins[None, :], axis=1).astype(jnp.float32)
    member = (
        (positions[:, None] >= begins[None, :]) & (positions[:, None] < ends[None, :])
    ).astype(jnp.float32)
    return (starts, member)


def advantages(rewards, prompts):
    same = (prompts[:, None] == prompts[None, :]).astype(jnp.float32)
    return rewards - jnp.sum(same * rewards[None, :], axis=1) / jnp.sum(same, axis=1)


def forward_chain(linear, offset, zero_state):

    def hop(step_index, incoming):
        outgoing = jnp.einsum("hvk,hkj->hvj", incoming, linear, precision=highest) + offset
        return from_behind(outgoing, "ctx", 1)

    return lax.fori_loop(0, lax.axis_size("ctx") - 1, hop, zero_state)


def backward_chain(linear, local_back, zero_state):
    flipped = jnp.swapaxes(linear, 1, 2)

    def back_hop(step_index, incoming):
        outgoing = jnp.einsum("hvk,hkj->hvj", incoming, flipped, precision=highest) + local_back
        return from_behind(outgoing, "ctx", -1)

    return lax.fori_loop(0, lax.axis_size("ctx") - 1, back_hop, zero_state)


def local(
    queries,
    key_rows,
    value_rows,
    hidden_in,
    beta_weight,
    log_gate,
    out_grad,
    lengths,
    rewards,
    prompts,
):
    token_count = queries.shape[0]
    heads = beta_weight.shape[1]
    width = queries.shape[1] // heads
    ctx_count = lax.axis_size("ctx")
    roll_count = lengths.shape[1]
    group_tokens = token_count * ctx_count
    positions = lax.axis_index("ctx") * token_count + jnp.arange(token_count, dtype=jnp.int32)
    starts, member = token_plan(lengths[0], positions)
    own_advantage = lax.dynamic_slice_in_dim(
        advantages(rewards, prompts), lax.axis_index("dp") * roll_count, roll_count
    )
    roll_weight = own_advantage * group_tokens / (roll_count * lengths[0].astype(jnp.float32))
    token_weight = jnp.sum(member * roll_weight[None, :], axis=-1)
    cotangent = out_grad.astype(jnp.float32) * token_weight[:, None]
    logits = jnp.dot(hidden_in, beta_weight, preferred_element_type=jnp.float32)
    query_f = queries.astype(jnp.float32)
    key_f = key_rows.astype(jnp.float32)
    value_f = value_rows.astype(jnp.float32)
    zero_state = jnp.zeros((heads, width, width), jnp.float32)

    def local_terms(a_rows, b_rows, c_rows, d_rows, e_rows):
        return segment_terms(a_rows, b_rows, c_rows, d_rows, e_rows, starts)

    terms, terms_back = jax.vjp(local_terms, query_f, key_f, value_f, logits, log_gate)
    linear, offset = segment_map(terms, zero_state)
    state_in = forward_chain(linear, offset, zero_state)
    unused, full_pull = jax.vjp(output_from_terms, terms, state_in)
    local_back = full_pull((cotangent, zero_state))[1]
    end_grad = backward_chain(linear, local_back, zero_state)
    term_grads = full_pull((cotangent, end_grad))[0]
    grads = terms_back(term_grads)
    logit_grad = grads[3]
    piece = hidden_in.astype(jnp.float32)
    beta_weight_grad = lax.psum_scatter(
        jnp.dot(piece.T, logit_grad, precision=highest, preferred_element_type=jnp.float32),
        ("dp", "ctx"),
        scatter_dimension=0,
        tiled=True,
    )
    return (
        grads[0].astype(jnp.bfloat16),
        grads[1].astype(jnp.bfloat16),
        grads[2].astype(jnp.bfloat16),
        grads[4],
        beta_weight_grad,
    )


def solution(mesh):
    in_specs = (
        P(("dp", "ctx"), None),
        P(("dp", "ctx"), None),
        P(("dp", "ctx"), None),
        P(("dp", "ctx"), None),
        P(),
        P(None, ("dp", "ctx")),
        P(("dp", "ctx"), None),
        P("dp", None),
        P(),
        P(),
    )
    out_specs = (
        P(("dp", "ctx"), None),
        P(("dp", "ctx"), None),
        P(("dp", "ctx"), None),
        P(None, ("dp", "ctx")),
        P(("dp", "ctx"), None),
    )
    return jax.shard_map(local, mesh=mesh, in_specs=in_specs, out_specs=out_specs, check_vma=False)
```

profile of v0, /device:TPU:0, one launch (start us, length us, event | category | flops | bytes accessed | tf_op | source)
XLA Modules:
  0.0 739.3 jit_solution(4360062447931801079)
XLA Ops:
  40.9 7.1 fusion.95
  48.0 5.6 multiply_subtract_fusion
  56.6 13.1 %while.86 = (s32[]{:T(128)}, f32[16,128,128]{1,2,0:T(8,128)S(1)}, f32[16,128,128]{1,2,0:T(8,128)}, f32[2,16,128,128]{2,3,1,0:T(8,128)}, f32[2,16,128,128]{2,3,1,0:T(8,128)}, /*index=5*/s32[]{:T(128)}, s32[]{:T(128)}) while((s32[]{:T(128)}, f32[16,128,128]{1,2,0:T(8,128)S(1)}, f32[16,128,128]{1,2,0:T(8,128)}, ...), condition=%wide.region_6.7_spmd.clone, body=%wide.region_5.6_spmd.clone.sunk | while | flops 805830656 | bytes 19924088 | solution.py:113
  74.8 204.0 %while.83 = (s32[]{:T(128)}, f32[16,128,128]{2,1,0:T(8,128)}, f32[16,128,128]{2,1,0:T(8,128)}, f32[16,128,128]{2,1,0:T(8,128)}, s32[]{:T(128)}) while((s32[]{:T(128)}, f32[16,128,128]{2,1,0:T(8,128)}, f32[16,128,128]{2,1,0:T(8,128)}, f32[16,128,128]{2,1,0:T(8,128)}, s32[]{:T(128)}) %tuple.180), condition=%wide.region_16.17_spmd, body=%wide.region_15.16_spmd.sunk | while | flops 402915328 | bytes 8388709 | solution.py:138
  78.8 5.9 collective-permute-start.1
  84.7 21.7 %collective-permute-done.1 = f32[16,128,128]{2,1,0:T(8,128)} collective-permute-done((f32[16,128,128]{2,1,0:T(8,128)}, f32[16,128,128]{2,1,0:T(8,128)}, u32[]{:S(2)}, u32[]{:S(2)}) %collective-permute-start.1) | collective-permute-done | bytes 1048608 | tf_op jit(solution)/shard_map/while/body/eval_jaxpr/ppermute | solution.py:15
  110.3 5.4 collective-permute-start.1
  115.7 20.8 %collective-permute-done.1 = f32[16,128,128]{2,1,0:T(8,128)} collective-permute-done((f32[16,128,128]{2,1,0:T(8,128)}, f32[16,128,128]{2,1,0:T(8,128)}, u32[]{:S(2)}, u32[]{:S(2)}) %collective-permute-start.1) | collective-permute-done | bytes 1048608 | tf_op jit(solution)/shard_map/while/body/eval_jaxpr/ppermute | solution.py:15
  140.5 5.4 collective-permute-start.1
  145.9 20.0 %collective-permute-done.1 = f32[16,128,128]{2,1,0:T(8,128)} collective-permute-done((f32[16,128,128]{2,1,0:T(8,128)}, f32[16,128,128]{2,1,0:T(8,128)}, u32[]{:S(2)}, u32[]{:S(2)}) %collective-permute-start.1) | collective-permute-done | bytes 1048608 | tf_op jit(solution)/shard_map/while/body/eval_jaxpr/ppermute | solution.py:15
  169.9 6.3 collective-permute-start.1
  176.2 19.1 %collective-permute-done.1 = f32[16,128,128]{2,1,0:T(8,128)} collective-permute-done((f32[16,128,128]{2,1,0:T(8,128)}, f32[16,128,128]{2,1,0:T(8,128)}, u32[]{:S(2)}, u32[]{:S(2)}) %collective-permute-start.1) | collective-permute-done | bytes 1048608 | tf_op jit(solution)/shard_map/while/body/eval_jaxpr/ppermute | solution.py:15
  199.3 6.3 collective-permute-start.1
  205.6 18.2 %collective-permute-done.1 = f32[16,128,128]{2,1,0:T(8,128)} collective-permute-done((f32[16,128,128]{2,1,0:T(8,128)}, f32[16,128,128]{2,1,0:T(8,128)}, u32[]{:S(2)}, u32[]{:S(2)}) %collective-permute-start.1) | collective-permute-done | bytes 1048608 | tf_op jit(solution)/shard_map/while/body/eval_jaxpr/ppermute | solution.py:15
  227.8 6.3 collective-permute-start.1
  234.1 17.4 %collective-permute-done.1 = f32[16,128,128]{2,1,0:T(8,128)} collective-permute-done((f32[16,128,128]{2,1,0:T(8,128)}, f32[16,128,128]{2,1,0:T(8,128)}, u32[]{:S(2)}, u32[]{:S(2)}) %collective-permute-start.1) | collective-permute-done | bytes 1048608 | tf_op jit(solution)/shard_map/while/body/eval_jaxpr/ppermute | solution.py:15
  255.5 6.3 collective-permute-start.1
  261.8 16.5 %collective-permute-done.1 = f32[16,128,128]{2,1,0:T(8,128)} collective-permute-done((f32[16,128,128]{2,1,0:T(8,128)}, f32[16,128,128]{2,1,0:T(8,128)}, u32[]{:S(2)}, u32[]{:S(2)}) %collective-permute-start.1) | collective-permute-done | bytes 1048608 | tf_op jit(solution)/shard_map/while/body/eval_jaxpr/ppermute | solution.py:15
  282.9 9.8 %while.84 = (s32[]{:T(128)}, f32[16,128,128]{1,2,0:T(8,128)}, f32[2,16,128,128]{2,3,1,0:T(8,128)}, f32[2,16,128,128]{2,3,1,0:T(8,128)}, f32[2,16,128,128]{2,3,1,0:T(8,128)}, /*index=5*/s32[]{:T(128)}) while((s32[]{:T(128)}, f32[16,128,128]{1,2,0:T(8,128)}, f32[2,16,128,128]{2,3,1,0:T(8,128)}, f32[2,16,128,128]{2,3,1,0:T(8,128)}, ...), condition=%wide.region_18.19_spmd, body=%wide.region_17.18_spmd.sunk | while | flops 402915328 | bytes 25167484 | solution.py:74
  304.6 11.2 %while.87 = (s32[]{:T(128)}, f32[16,128,128]{1,2,0:T(8,128)}, f32[2,16,128,128]{3,2,1,0:T(8,128)}, f32[2,16,64,128]{3,2,1,0:T(8,128)}, f32[2,16,64,128]{3,2,1,0:T(8,128)}, /*index=5*/s32[]{:T(128)}, s32[]{:T(128)}) while((s32[]{:T(128)}, f32[16,128,128]{1,2,0:T(8,128)}, f32[2,16,128,128]{3,2,1,0:T(8,128)}, ...), condition=%wide.region_12.13_spmd.clone, body=%wide.region_11.12_spmd.clone.sunk | while | flops 604504064 | bytes 14681247 | solution.py:74
  319.5 168.4 %while.82 = (s32[]{:T(128)}, f32[16,128,128]{2,1,0:T(8,128)}, f32[16,128,128]{2,1,0:T(8,128)S(1)}, f32[16,128,128]{2,1,0:T(8,128)}, s32[]{:T(128)}) while((s32[]{:T(128)}, f32[16,128,128]{2,1,0:T(8,128)}, f32[16,128,128]{2,1,0:T(8,128)S(1)}, f32[16,128,128]{2,1,0:T(8,128)}, s32[]{:T(128)}) %tuple.192), condition=%wide.region_14.15_spmd, body=%wide.region_13.14_spmd.sunk | while | flops 402915328 | bytes 8388709 | solution.py:148
  324.5 21.5 %collective-permute-done = f32[16,128,128]{2,1,0:T(8,128)} collective-permute-done((f32[16,128,128]{2,1,0:T(8,128)}, f32[16,128,128]{2,1,0:T(8,128)}, u32[]{:S(2)}, u32[]{:S(2)}) %collective-permute-start) | collective-permute-done | bytes 1048608 | tf_op jit(solution)/shard_map/while/body/eval_jaxpr/ppermute | solution.py:15
  351.1 20.9 %collective-permute-done = f32[16,128,128]{2,1,0:T(8,128)} collective-permute-done((f32[16,128,128]{2,1,0:T(8,128)}, f32[16,128,128]{2,1,0:T(8,128)}, u32[]{:S(2)}, u32[]{:S(2)}) %collective-permute-start) | collective-permute-done | bytes 1048608 | tf_op jit(solution)/shard_map/while/body/eval_jaxpr/ppermute | solution.py:15
  377.0 19.3 %collective-permute-done = f32[16,128,128]{2,1,0:T(8,128)} collective-permute-done((f32[16,128,128]{2,1,0:T(8,128)}, f32[16,128,128]{2,1,0:T(8,128)}, u32[]{:S(2)}, u32[]{:S(2)}) %collective-permute-start) | collective-permute-done | bytes 1048608 | tf_op jit(solution)/shard_map/while/body/eval_jaxpr/ppermute | solution.py:15
  401.4 18.4 %collective-permute-done = f32[16,128,128]{2,1,0:T(8,128)} collective-permute-done((f32[16,128,128]{2,1,0:T(8,128)}, f32[16,128,128]{2,1,0:T(8,128)}, u32[]{:S(2)}, u32[]{:S(2)}) %collective-permute-start) | collective-permute-done | bytes 1048608 | tf_op jit(solution)/shard_map/while/body/eval_jaxpr/ppermute | solution.py:15
  424.8 18.3 %collective-permute-done = f32[16,128,128]{2,1,0:T(8,128)} collective-permute-done((f32[16,128,128]{2,1,0:T(8,128)}, f32[16,128,128]{2,1,0:T(8,128)}, u32[]{:S(2)}, u32[]{:S(2)}) %collective-permute-start) | collective-permute-done | bytes 1048608 | tf_op jit(solution)/shard_map/while/body/eval_jaxpr/ppermute | solution.py:15
  448.2 18.3 %collective-permute-done = f32[16,128,128]{2,1,0:T(8,128)} collective-permute-done((f32[16,128,128]{2,1,0:T(8,128)}, f32[16,128,128]{2,1,0:T(8,128)}, u32[]{:S(2)}, u32[]{:S(2)}) %collective-permute-start) | collective-permute-done | bytes 1048608 | tf_op jit(solution)/shard_map/while/body/eval_jaxpr/ppermute | solution.py:15
  471.5 16.3 %collective-permute-done = f32[16,128,128]{2,1,0:T(8,128)} collective-permute-done((f32[16,128,128]{2,1,0:T(8,128)}, f32[16,128,128]{2,1,0:T(8,128)}, u32[]{:S(2)}, u32[]{:S(2)}) %collective-permute-start) | collective-permute-done | bytes 1048608 | tf_op jit(solution)/shard_map/while/body/eval_jaxpr/ppermute | solution.py:15
  494.9 26.4 %while.85 = (s32[]{:T(128)}, f32[16,128,128]{1,2,0:T(8,128)S(1)}, f32[2,16,64,128]{3,2,1,0:T(8,128)}, f32[2,16,64,128]{3,2,1,0:T(8,128)}, f32[2,16,128,128]{2,3,...) while((s32[]{:T(128)}, f32[16,128,128]{1,2,0:T(8,128)S(1)}, ...), condition=%wide.region_20.21_spmd, body=%wide.region_19.20_spmd.sunk | while | flops 1208221696 | bytes 65015652 | solution.py:74
  521.2 6.2 fusion.167
  606.6 5.7 multiply_reduce_fusion.4
  624.9 105.8 %all-reduce.5.cloned.1.call-done = f32[2304,16]{0,1:T(8,128)} async-done(((f32[2304,16]{0,1:T(8,128)}), f32[2304,16]{0,1:T(8,128)}) %all-reduce.5.cloned.1.call-update) | async-done | bytes 147472
  (345 shorter events, 283.6 us)
Async XLA Ops:
  7.2 723.5 %all-reduce.5.cloned.1.call-start = ((), (), s32[]{:S(2)}) async-start(), calls=%async_computation | async-start | bytes 294912
  16.1 4.2 copy-start.23
  40.8 7.2 copy-start.20
  78.8 27.6 %collective-permute-start.1 = (f32[16,128,128]{2,1,0:T(8,128)}, f32[16,128,128]{2,1,0:T(8,128)}, u32[]{:S(2)}, u32[]{:S(2)}) collective-permute-start(f32[16,128,128]{2,1,0:T(8,128)} %convolution_add_fusion.31), channel_id=1, source_target_pairs={{0,1},{1,2},{2,3},{3,4},{4,5},{5,6},{6,7},{8,9},{9,10},{10,11},{11... | collective-permute-start | bytes 3145736 | tf_op jit(solution)/shard_map/while/body/eval_jaxpr/ppermute | solution.py:15
  110.3 26.2 %collective-permute-start.1 = (f32[16,128,128]{2,1,0:T(8,128)}, f32[16,128,128]{2,1,0:T(8,128)}, u32[]{:S(2)}, u32[]{:S(2)}) collective-permute-start(f32[16,128,128]{2,1,0:T(8,128)} %convolution_add_fusion.31), channel_id=1, source_target_pairs={{0,1},{1,2},{2,3},{3,4},{4,5},{5,6},{6,7},{8,9},{9,10},{10,11},{11... | collective-permute-start | bytes 3145736 | tf_op jit(solution)/shard_map/while/body/eval_jaxpr/ppermute | solution.py:15
  140.5 25.4 %collective-permute-start.1 = (f32[16,128,128]{2,1,0:T(8,128)}, f32[16,128,128]{2,1,0:T(8,128)}, u32[]{:S(2)}, u32[]{:S(2)}) collective-permute-start(f32[16,128,128]{2,1,0:T(8,128)} %convolution_add_fusion.31), channel_id=1, source_target_pairs={{0,1},{1,2},{2,3},{3,4},{4,5},{5,6},{6,7},{8,9},{9,10},{10,11},{11... | collective-permute-start | bytes 3145736 | tf_op jit(solution)/shard_map/while/body/eval_jaxpr/ppermute | solution.py:15
  169.9 25.4 %collective-permute-start.1 = (f32[16,128,128]{2,1,0:T(8,128)}, f32[16,128,128]{2,1,0:T(8,128)}, u32[]{:S(2)}, u32[]{:S(2)}) collective-permute-start(f32[16,128,128]{2,1,0:T(8,128)} %convolution_add_fusion.31), channel_id=1, source_target_pairs={{0,1},{1,2},{2,3},{3,4},{4,5},{5,6},{6,7},{8,9},{9,10},{10,11},{11... | collective-permute-start | bytes 3145736 | tf_op jit(solution)/shard_map/while/body/eval_jaxpr/ppermute | solution.py:15
  199.3 24.6 %collective-permute-start.1 = (f32[16,128,128]{2,1,0:T(8,128)}, f32[16,128,128]{2,1,0:T(8,128)}, u32[]{:S(2)}, u32[]{:S(2)}) collective-permute-start(f32[16,128,128]{2,1,0:T(8,128)} %convolution_add_fusion.31), channel_id=1, source_target_pairs={{0,1},{1,2},{2,3},{3,4},{4,5},{5,6},{6,7},{8,9},{9,10},{10,11},{11... | collective-permute-start | bytes 3145736 | tf_op jit(solution)/shard_map/while/body/eval_jaxpr/ppermute | solution.py:15
  227.8 23.7 %collective-permute-start.1 = (f32[16,128,128]{2,1,0:T(8,128)}, f32[16,128,128]{2,1,0:T(8,128)}, u32[]{:S(2)}, u32[]{:S(2)}) collective-permute-start(f32[16,128,128]{2,1,0:T(8,128)} %convolution_add_fusion.31), channel_id=1, source_target_pairs={{0,1},{1,2},{2,3},{3,4},{4,5},{5,6},{6,7},{8,9},{9,10},{10,11},{11... | collective-permute-start | bytes 3145736 | tf_op jit(solution)/shard_map/while/body/eval_jaxpr/ppermute | solution.py:15
  255.5 22.9 %collective-permute-start.1 = (f32[16,128,128]{2,1,0:T(8,128)}, f32[16,128,128]{2,1,0:T(8,128)}, u32[]{:S(2)}, u32[]{:S(2)}) collective-permute-start(f32[16,128,128]{2,1,0:T(8,128)} %convolution_add_fusion.31), channel_id=1, source_target_pairs={{0,1},{1,2},{2,3},{3,4},{4,5},{5,6},{6,7},{8,9},{9,10},{10,11},{11... | collective-permute-start | bytes 3145736 | tf_op jit(solution)/shard_map/while/body/eval_jaxpr/ppermute | solution.py:15
  294.1 3.8 copy-start.21
  297.9 3.8 copy-start.67
  323.2 22.8 %collective-permute-start = (f32[16,128,128]{2,1,0:T(8,128)}, f32[16,128,128]{2,1,0:T(8,128)}, u32[]{:S(2)}, u32[]{:S(2)}) collective-permute-start(f32[16,128,128]{2,1,0:T(8,128)} %convolution_add_fusion.30), channel_id=1, source_target_pairs={{1,0},{2,1},{3,2},{4,3},{5,4},{6,5},{7,6},{9,8},{10,9},{11,10},{12... | collective-permute-start | bytes 3145736 | tf_op jit(solution)/shard_map/while/body/eval_jaxpr/ppermute | solution.py:15
  349.8 22.2 %collective-permute-start = (f32[16,128,128]{2,1,0:T(8,128)}, f32[16,128,128]{2,1,0:T(8,128)}, u32[]{:S(2)}, u32[]{:S(2)}) collective-permute-start(f32[16,128,128]{2,1,0:T(8,128)} %convolution_add_fusion.30), channel_id=1, source_target_pairs={{1,0},{2,1},{3,2},{4,3},{5,4},{6,5},{7,6},{9,8},{10,9},{11,10},{12... | collective-permute-start | bytes 3145736 | tf_op jit(solution)/shard_map/while/body/eval_jaxpr/ppermute | solution.py:15
  375.7 20.6 %collective-permute-start = (f32[16,128,128]{2,1,0:T(8,128)}, f32[16,128,128]{2,1,0:T(8,128)}, u32[]{:S(2)}, u32[]{:S(2)}) collective-permute-start(f32[16,128,128]{2,1,0:T(8,128)} %convolution_add_fusion.30), channel_id=1, source_target_pairs={{1,0},{2,1},{3,2},{4,3},{5,4},{6,5},{7,6},{9,8},{10,9},{11,10},{12... | collective-permute-start | bytes 3145736 | tf_op jit(solution)/shard_map/while/body/eval_jaxpr/ppermute | solution.py:15
  400.1 19.7 %collective-permute-start = (f32[16,128,128]{2,1,0:T(8,128)}, f32[16,128,128]{2,1,0:T(8,128)}, u32[]{:S(2)}, u32[]{:S(2)}) collective-permute-start(f32[16,128,128]{2,1,0:T(8,128)} %convolution_add_fusion.30), channel_id=1, source_target_pairs={{1,0},{2,1},{3,2},{4,3},{5,4},{6,5},{7,6},{9,8},{10,9},{11,10},{12... | collective-permute-start | bytes 3145736 | tf_op jit(solution)/shard_map/while/body/eval_jaxpr/ppermute | solution.py:15
  423.6 19.6 %collective-permute-start = (f32[16,128,128]{2,1,0:T(8,128)}, f32[16,128,128]{2,1,0:T(8,128)}, u32[]{:S(2)}, u32[]{:S(2)}) collective-permute-start(f32[16,128,128]{2,1,0:T(8,128)} %convolution_add_fusion.30), channel_id=1, source_target_pairs={{1,0},{2,1},{3,2},{4,3},{5,4},{6,5},{7,6},{9,8},{10,9},{11,10},{12... | collective-permute-start | bytes 3145736 | tf_op jit(solution)/shard_map/while/body/eval_jaxpr/ppermute | solution.py:15
  446.9 19.6 %collective-permute-start = (f32[16,128,128]{2,1,0:T(8,128)}, f32[16,128,128]{2,1,0:T(8,128)}, u32[]{:S(2)}, u32[]{:S(2)}) collective-permute-start(f32[16,128,128]{2,1,0:T(8,128)} %convolution_add_fusion.30), channel_id=1, source_target_pairs={{1,0},{2,1},{3,2},{4,3},{5,4},{6,5},{7,6},{9,8},{10,9},{11,10},{12... | collective-permute-start | bytes 3145736 | tf_op jit(solution)/shard_map/while/body/eval_jaxpr/ppermute | solution.py:15
  470.2 17.6 %collective-permute-start = (f32[16,128,128]{2,1,0:T(8,128)}, f32[16,128,128]{2,1,0:T(8,128)}, u32[]{:S(2)}, u32[]{:S(2)}) collective-permute-start(f32[16,128,128]{2,1,0:T(8,128)} %convolution_add_fusion.30), channel_id=1, source_target_pairs={{1,0},{2,1},{3,2},{4,3},{5,4},{6,5},{7,6},{9,8},{10,9},{11,10},{12... | collective-permute-start | bytes 3145736 | tf_op jit(solution)/shard_map/while/body/eval_jaxpr/ppermute | solution.py:15
  494.9 4.7 copy-start.5
  501.2 4.9 copy-start.33
  508.0 4.6 copy-start.5
  514.3 4.9 copy-start.33
  521.2 6.2 copy-start.34
  579.2 4.6 copy-start.35
  581.1 13.0 %copy-start.54 = (f32[2,16,64,128]{3,2,1,0:T(8,128)}, f32[2,16,64,128]{3,2,1,0:T(8,128)S(1)}, u32[]{:S(2)}) copy-start(f32[2,16,64,128]{3,2,1,0:T(8,128)S(1)} %fusion.102) | copy-start | bytes 3145732
  583.8 10.3 %copy-start.56 = (f32[2,16,64,128]{3,2,1,0:T(8,128)}, f32[2,16,64,128]{3,2,1,0:T(8,128)S(1)}, u32[]{:S(2)}) copy-start(f32[2,16,64,128]{3,2,1,0:T(8,128)S(1)} %fusion.100) | copy-start | bytes 3145732
  587.8 6.3 copy-start.58
  587.8 4.5 copy-start.15
  599.3 4.4 copy-start.27
  599.3 4.4 copy-start.53
  606.6 5.8 copy-start.19
  (64 other events, 148.2 us)
Sparse Core Ops, SparseCore 0:
  606.7 123.8 all-reduce.4
where the time goes:
time: 752 us; the launch traced here: 739 us
  waiting for transfers between devices  372 us (49%)
  matrix products  226 us (30%)
  local copies, waits for them, and re-layouts  54 us (7%)
  starting transfers between devices  51 us (7%)
  other arithmetic  19.2 us (3%)
  between operations  15.7 us (2%)
    ppermute x14, waiting for transfers between devices, from_behind(): return lax.ppermute(x, axis, pairs)  267 us
    unnamed x2, waiting for transfers between devices  106 us
    ppermute x14, starting transfers between devices, from_behind(): return lax.ppermute(x, axis, pairs)  51 us
    dot_general x7, matrix products, hop(): jnp.einsum('hvk,hkj->hvj', incoming, linear, precision=highest) + offset  27.8 us
    dot_general x15, matrix products, unit_inverse(): power = jnp.einsum('nhij,nhjk->nhik', power, power, precision=highest)  27.3 us
    dot_general x7, matrix products, back_hop(): jnp.einsum('hvk,hkj->hvj', incoming, flipped, precision=highest)  26.4 us
    dot_general x15, matrix products, unit_inverse(): jnp.einsum('nhij,nhjk->nhik', total, power, precision=highest)  25.8 us
    dot_general x8, matrix products, advance(): jnp.einsum('hvk,hkj->hvj', state, piece_map, precision=highest)  21.3 us
  transfers between devices with their start and end apart: 15, of which 15 were waited for; matrix products, arithmetic and copies ran while one was open for 2% of the time, Pallas kernels for 0%

commit v1 on v0

v1 whole, which is shorter than its diff:
```python
import functools

import jax
import jax.numpy as jnp
from jax import lax
from jax.experimental import pallas as pl
from jax.experimental.pallas import tpu as pltpu
from jax.sharding import PartitionSpec as P

PACK = 2
SMALL = 16
highest = lax.Precision.HIGHEST
MESH = pl.DeviceIdType.MESH
F32 = jnp.float32
BF16 = jnp.bfloat16


def split(x):
    hi = x.astype(BF16)
    return hi, (x - hi.astype(F32)).astype(BF16)


def left(x):
    return jnp.concatenate(split(x), axis=1)


def left_t(x):
    return jnp.concatenate(split(x), axis=0)


def right(x):
    row = jnp.concatenate(split(x), axis=1)
    return jnp.concatenate([row, row], axis=0)


def right_t(x):
    hi, lo = split(x)
    return jnp.concatenate(
        [jnp.concatenate([hi, hi], axis=1), jnp.concatenate([lo, lo], axis=1)], axis=0
    )


def contract(a, b, dims):
    out = lax.dot_general(a, b, ((dims[:1], dims[1:]), ((), ())), preferred_element_type=F32)
    half = out.shape[1] // 2
    return out[:, :half] + out[:, half:]


def mul(a, b):
    return contract(left(a), right(b), (1, 0))


def mul_t(a, b):
    return contract(left(a), right_t(b), (1, 1))


def t_mul(a, b):
    return contract(left_t(a), right(b), (0, 0))


def stack(*parts):
    return jnp.concatenate(parts, axis=0)


def row_sum(x):
    return jnp.sum(x, axis=1, keepdims=True)


def inverses(lows, rows, cols):
    size = lows[0].shape[0]
    eye = jnp.where(rows == cols, 1.0, 0.0)
    base = min(SMALL, size)
    same = (rows // base) == (cols // base)
    powers = [jnp.where(same, -low, 0.0) for low in lows]
    totals = [eye + power for power in powers]
    powers = [mul(power, power) for power in powers]
    reach = 2
    while reach * 2 < base:
        both = [mul(stack(t, p), p) for t, p in zip(totals, powers)]
        totals = [t + b[:size] for t, b in zip(totals, both)]
        powers = [b[size:] for b in both]
        reach *= 2
    totals = [t + mul(t, p) for t, p in zip(totals, powers)]
    while base < size:
        own = ((rows // (2 * base)) == (cols // (2 * base))) & ((rows // base) != (cols // base))
        parts = [jnp.where(own, low, 0.0) for low in lows]
        mids = [mul(t, part) for t, part in zip(totals, parts)]
        totals = [t - mul(m, t) for t, m in zip(totals, mids)]
        base *= 2
    return totals


def kernel(
    q_ref, k_ref, v_ref, o_ref, cols_ref, rows_ref,
    dq_ref, dk_ref, dv_ref, dgate_ref, dlogit_ref,
    inv_ref, mix_ref, dkk_ref, dec_ref, map_ref, fout_ref, bout_ref, fin_ref, bin_ref,
    fsend, frecv, bsend, brecv,
):
    tokens = q_ref.shape[0]
    groups = cols_ref.shape[0]
    width = fin_ref.shape[-1]
    count = lax.axis_size("ctx")
    seg = lax.axis_index("ctx")
    last = count - 1

    barrier = pltpu.get_barrier_semaphore()

    @pl.when(seg > 0)
    def _():
        pl.semaphore_signal(barrier, inc=1, device_id={"ctx": seg - 1}, device_id_type=MESH)

    @pl.when(seg < last)
    def _():
        pl.semaphore_signal(barrier, inc=1, device_id={"ctx": seg + 1}, device_id_type=MESH)

    pl.semaphore_wait(barrier, jnp.minimum(seg, 1) + jnp.minimum(last - seg, 1))

    def forward_copy(group):
        return pltpu.make_async_remote_copy(
            src_ref=fout_ref.at[group], dst_ref=fin_ref.at[group],
            send_sem=fsend.at[group], recv_sem=frecv.at[group],
            device_id={"ctx": seg + 1}, device_id_type=MESH,
        )

    def backward_copy(group):
        return pltpu.make_async_remote_copy(
            src_ref=bout_ref.at[group], dst_ref=bin_ref.at[group],
            send_sem=bsend.at[group], recv_sem=brecv.at[group],
            device_id={"ctx": seg - 1}, device_id_type=MESH,
        )

    rows = lax.broadcasted_iota(jnp.int32, (tokens, tokens), 0)
    cols = lax.broadcasted_iota(jnp.int32, (tokens, tokens), 1)
    heads = range(PACK)

    def lanes(group, i):
        return pl.ds(pl.multiple_of((group * PACK + i) * width, width), width)

    def load(ref, group, i):
        return ref[:, lanes(group, i)].astype(F32)

    def token_columns(group, i):
        block = cols_ref[group]
        row_block = rows_ref[group]
        beta = block[:, i:i + 1]
        gamma = block[:, PACK + i:PACK + i + 1]
        number = block[:, 2 * PACK:2 * PACK + 1]
        weight = block[:, 2 * PACK + 1:2 * PACK + 2]
        gamma_row = row_block[i:i + 1, :]
        number_row = row_block[PACK:PACK + 1, :]
        head = jnp.where(number == 0.0, jnp.exp(gamma), 0.0)
        tied = number == number_row[:, tokens - 1:tokens]
        tail = jnp.where(
            tied, jnp.exp(jnp.where(tied, gamma_row[:, tokens - 1:tokens] - gamma, 0.0)), 0.0
        )
        return beta, gamma, number, weight, gamma_row, number_row, head, tail

    def scales(x):
        return lax.rsqrt(row_sum(x * x) + 1e-06)

    def local_part(group):
        lows, keep = [], []
        for i in heads:
            beta, gamma, number, weight, gamma_row, number_row, head, tail = token_columns(group, i)
            q, k = load(q_ref, group, i), load(k_ref, group, i)
            qh, kh = q * scales(q), k * scales(k)
            linked = (number == number_row) & (rows >= cols)
            decay = jnp.where(linked, jnp.exp(jnp.where(linked, gamma - gamma_row, 0.0)), 0.0)
            both = mul_t(stack(kh, qh), kh)
            dkk = jnp.where(rows > cols, decay * both[:tokens], 0.0)
            mix = decay * both[tokens:]
            dec_ref[group, i] = decay
            dkk_ref[group, i] = dkk
            mix_ref[group, i] = mix
            lows.append(beta * dkk)
            keep.append((beta, weight, head, tail, qh, kh, mix))
        invs = inverses(lows, rows, cols)
        for i in heads:
            inv_ref[group, i] = invs[i]
        pairs = []
        for i in heads:
            beta, weight, head, tail, qh, kh, mix = keep[i]
            v = load(v_ref, group, i)
            pairs.append(mul(invs[i], jnp.concatenate([beta * v, (beta * head) * kh], axis=1)))
        eye = jnp.where(rows == cols, 1.0, 0.0)
        for i in heads:
            beta, weight, head, tail, qh, kh, mix = keep[i]
            z = pairs[i][:, width:]
            ends = t_mul(pairs[i], tail * kh)
            fout_ref[group, i] = ends[:width]
            map_ref[group, i] = head[tokens - 1:tokens, :] * eye - ends[width:]
            carry = head * qh - mul(mix, z)
            bout_ref[group, i] = t_mul(load(o_ref, group, i) * weight, carry)

    def forward_hop(group):
        @pl.when(seg == 0)
        def _():
            fin_ref[group] = jnp.zeros_like(fin_ref[group])

        @pl.when(seg > 0)
        def _():
            forward_copy(group).wait_recv()

        @pl.when((seg > 0) & (seg < last))
        def _():
            for i in heads:
                fout_ref[group, i] = fout_ref[group, i] + mul(fin_ref[group, i], map_ref[group, i])

        @pl.when(seg < last)
        def _():
            forward_copy(group).start()

    def backward_hop(group):
        @pl.when(seg == last)
        def _():
            bin_ref[group] = jnp.zeros_like(bin_ref[group])

        @pl.when(seg < last)
        def _():
            backward_copy(group).wait_recv()

        @pl.when((seg > 0) & (seg < last))
        def _():
            for i in heads:
                bout_ref[group, i] = bout_ref[group, i] + mul_t(bin_ref[group, i], map_ref[group, i])

        @pl.when(seg > 0)
        def _():
            backward_copy(group).start()

    def gradient_part(group):
        upper = jnp.where(rows < cols, 1.0, 0.0).astype(BF16)
        upper = stack(upper, upper)
        keep = []
        for i in heads:
            beta, gamma, number, weight, gamma_row, number_row, head, tail = token_columns(group, i)
            q, k = load(q_ref, group, i), load(k_ref, group, i)
            qs, ks = scales(q), scales(k)
            qh, kh = q * qs, k * ks
            state = fin_ref[group, i]
            both = mul_t(stack(qh, kh), state)
            keep.append((beta, weight, head, tail, qs, ks, qh, kh, state, both[:tokens], both[tokens:]))
        rests = [load(v_ref, group, i) - keep[i][2] * keep[i][10] for i in heads]
        us = [mul(inv_ref[group, i], keep[i][0] * rests[i]) for i in heads]
        dos = [load(o_ref, group, i) * keep[i][1] for i in heads]
        dus = [
            t_mul(mix_ref[group, i], dos[i]) + mul_t(keep[i][3] * keep[i][7], bin_ref[group, i])
            for i in heads
        ]
        drs = [t_mul(inv_ref[group, i], dus[i]) for i in heads]
        squares = [mul_t(stack(dos[i], drs[i]), us[i]) for i in heads]
        logit_columns = []
        for i in heads:
            beta, weight, head, tail, qs, ks, qh, kh, state, qstate, kstate = keep[i]
            u, do, dr, rest, after = us[i], dos[i], drs[i], rests[i], bin_ref[group, i]
            decay, dkk = dec_ref[group, i], dkk_ref[group, i]
            dmix = squares[i][:tokens]
            dlow = jnp.where(rows > cols, -squares[i][tokens:], 0.0)
            inward = mul(stack(head * do, (-beta * head) * dr), state)
            uafter = mul(u, after)
            da = dmix * decay
            dpair = dlow * (beta * decay)
            pairs = stack(da, dpair)
            direct = mul(pairs, kh)
            turned = t_mul(pairs, stack(qh, kh))
            dqh = inward[:tokens] + direct[:tokens]
            dkh = inward[tokens:] + direct[tokens:] + turned + tail * uafter
            dq_ref[:, lanes(group, i)] = (qs * (dqh - qh * row_sum(qh * dqh))).astype(BF16)
            dk_ref[:, lanes(group, i)] = (ks * (dkh - kh * row_sum(kh * dkh))).astype(BF16)
            dv_ref[:, lanes(group, i)] = (beta * dr).astype(BF16)
            lowpart = dlow * dkk
            spread = dmix * mix_ref[group, i] + beta * lowpart
            across = lax.dot_general(
                left(spread), upper, (((1,), (0,)), ((), ())), preferred_element_type=F32
            )
            total = jnp.sum(row_sum(after * state), axis=0, keepdims=True)
            headgrad = row_sum(do * qstate) - beta * row_sum(dr * kstate)
            headgrad = head * (headgrad + jnp.where(rows[:, :1] == tokens - 1, total, 0.0))
            tailgrad = tail * row_sum(kh * uafter)
            dgate_ref[group, i:i + 1, :] = jnp.sum(
                jnp.where(rows >= cols, across + headgrad, tailgrad), axis=0, keepdims=True
            )
            dbeta = row_sum(dr * rest) + row_sum(lowpart)
            logit_columns.append(dbeta * beta * (1.0 - beta))
        dlogit_ref[group] = jnp.concatenate(logit_columns, axis=1)

    def step(t, unused):
        @pl.when(t < groups)
        def _():
            local_part(t)

        f = t - seg

        @pl.when((f >= 0) & (f < groups))
        def _():
            forward_hop(f)

        b = t - (last - seg)

        @pl.when((b >= 0) & (b < groups))
        def _():
            backward_hop(b)

        @pl.when(t >= last)
        def _():
            gradient_part(t - last)

        return unused

    lax.fori_loop(0, groups + last, step, 0)

    def drain(group, unused):
        @pl.when(seg < last)
        def _():
            forward_copy(group).wait_send()

        @pl.when(seg > 0)
        def _():
            backward_copy(group).wait_send()

        return unused

    lax.fori_loop(0, groups, drain, 0)


def token_plan(row_lengths, positions):
    ends = jnp.cumsum(row_lengths)
    begins = ends - row_lengths
    starts = jnp.any(positions[:, None] == begins[None, :], axis=1).astype(jnp.float32)
    member = (
        (positions[:, None] >= begins[None, :]) & (positions[:, None] < ends[None, :])
    ).astype(jnp.float32)
    return (starts, member)


def advantages(rewards, prompts):
    same = (prompts[:, None] == prompts[None, :]).astype(jnp.float32)
    return rewards - jnp.sum(same * rewards[None, :], axis=1) / jnp.sum(same, axis=1)


def local(
    queries, key_rows, value_rows, hidden_in, beta_weight, log_gate, out_grad,
    lengths, rewards, prompts,
):
    tokens = queries.shape[0]
    heads = beta_weight.shape[1]
    width = queries.shape[1] // heads
    groups = heads // PACK
    ctx_count = lax.axis_size("ctx")
    roll_count = lengths.shape[1]
    group_tokens = tokens * ctx_count
    positions = lax.axis_index("ctx") * tokens + jnp.arange(tokens, dtype=jnp.int32)
    starts, member = token_plan(lengths[0], positions)
    own_advantage = lax.dynamic_slice_in_dim(
        advantages(rewards, prompts), lax.axis_index("dp") * roll_count, roll_count
    )
    roll_weight = own_advantage * group_tokens / (roll_count * lengths[0].astype(jnp.float32))
    token_weight = jnp.sum(member * roll_weight[None, :], axis=-1)
    logits = jnp.dot(hidden_in, beta_weight, preferred_element_type=jnp.float32)
    beta = jax.nn.sigmoid(logits)
    gamma = jnp.cumsum(log_gate, axis=-1)
    number = jnp.cumsum(starts)
    shared = jnp.broadcast_to(
        jnp.stack([number, token_weight], axis=1)[None], (groups, tokens, 2)
    )
    columns = jnp.concatenate(
        [
            beta.reshape(tokens, groups, PACK).transpose(1, 0, 2),
            gamma.reshape(groups, PACK, tokens).transpose(0, 2, 1),
            shared,
        ],
        axis=2,
    )
    lines = jnp.concatenate(
        [
            gamma.reshape(groups, PACK, tokens),
            jnp.broadcast_to(number[None, None], (groups, 1, tokens)),
        ],
        axis=1,
    )
    square = (groups, PACK, tokens, tokens)
    states = (groups, PACK, width, width)
    vmem = pl.BlockSpec(memory_space=pltpu.VMEM)
    dq, dk, dv, dgate, dlogit = pl.pallas_call(
        kernel,
        out_shape=(
            jax.ShapeDtypeStruct(queries.shape, BF16),
            jax.ShapeDtypeStruct(queries.shape, BF16),
            jax.ShapeDtypeStruct(queries.shape, BF16),
            jax.ShapeDtypeStruct((groups, PACK, tokens), F32),
            jax.ShapeDtypeStruct((groups, tokens, PACK), F32),
        ),
        in_specs=[vmem] * 6,
        out_specs=(vmem,) * 5,
        scratch_shapes=[pltpu.VMEM(square, F32)] * 4
        + [pltpu.VMEM(states, F32)] * 5
        + [pltpu.SemaphoreType.DMA((groups,))] * 4,
        compiler_params=pltpu.CompilerParams(
            collective_id=0, has_side_effects=True, vmem_limit_bytes=48 * 2**20
        ),
        name="delta_backward",
    )(queries, key_rows, value_rows, out_grad, columns, lines)
    logit_grad = dlogit.transpose(1, 0, 2).reshape(tokens, heads)
    piece = hidden_in.astype(jnp.float32)
    beta_weight_grad = lax.psum_scatter(
        jnp.dot(piece.T, logit_grad, precision=highest, preferred_element_type=jnp.float32),
        ("dp", "ctx"),
        scatter_dimension=0,
        tiled=True,
    )
    return (dq, dk, dv, dgate.reshape(heads, tokens), beta_weight_grad)


def solution(mesh):
    rows = P(("dp", "ctx"), None)
    in_specs = (
        rows, rows, rows, rows, P(), P(None, ("dp", "ctx")), rows, P("dp", None), P(), P(),
    )
    out_specs = (rows, rows, rows, P(None, ("dp", "ctx")), rows)
    return jax.shard_map(local, mesh=mesh, in_specs=in_specs, out_specs=out_specs, check_vma=False)
```

time: 752 us -> 232 us (0.31); the launches traced: 739 us -> 230 us
  waiting for transfers between devices: 372 us -> 120 us
  matrix products: 226 us -> 1.27 us
  Pallas kernels: 0 us -> 83.7 us
  starting transfers between devices: 51 us -> 0.04 us
  local copies, waits for them, and re-layouts: 54 us -> 9.23 us
  other arithmetic: 19.2 us -> 1.92 us
    ppermute x14 -> x0, waiting for transfers between devices: 267 us -> none  [from_behind(): return lax.ppermute(x, axis, pairs)]
    dot_general x85 -> x0, matrix products: 224 us -> none  [the longest x7 27.8 us: hop(): jnp.einsum('hvk,hkj->hvj', incoming, linear, precision=highest) + offset]
    pallas_call x0 -> x1, Pallas kernels: none -> 83.7 us  [local(): pl.pallas_call(kernel, out_shape=(jax.ShapeDtypeStruct(queries.shape, BF1...]
    ppermute x14 -> x0, starting transfers between devices: 51 us -> none  [from_behind(): return lax.ppermute(x, axis, pairs)]
    while x63 -> x0, local copies, waits for them, and re-layouts: 22.5 us -> none
    unnamed x2, waiting for transfers between devices: 106 us -> 120 us
  transfers between devices with their start and end apart: 15 -> 1, of which waited for: 15 -> 1; matrix products, arithmetic and copies ran while one was open for 2% -> 0% of each run, Pallas kernels for 0% -> 0%
where the time goes in v1:
time: 232 us; the launch traced here: 230 us
  waiting for transfers between devices  120 us (52%)
  Pallas kernels  83.7 us (36%)
  between operations  14.2 us (6%)
  local copies, waits for them, and re-layouts  9.23 us (4%)
    unnamed x2, waiting for transfers between devices  120 us
    pallas_call x1, Pallas kernels, local(): pl.pallas_call(kernel, out_shape=(jax.ShapeDtypeStruct(queries.shape, BF1...  83.7 us
    unnamed x23, local copies, waits for them, and re-layouts  7.52 us
  transfers between devices with their start and end apart: 1, of which 1 were waited for; matrix products, arithmetic and copies ran while one was open for 0% of the time, Pallas kernels for 0%

profile of v1, /device:TPU:0, one launch (start us, length us, event | category | flops | bytes accessed | tf_op | source)
XLA Modules:
  0.0 230.0 jit_solution(4045697419997150817)
XLA Ops:
  7.2 0.8 copy.43
  8.0 0.6 reduce_window_sum.28
  8.5 0.2 copy.44
  8.8 0.6 copy-done.8
  9.5 0.2 reduce-window.6
  9.7 0.7 copy-done.7
  10.3 0.2 fusion.4
  10.5 0.1 bitcast_divide_fusion
  10.6 0.1 compare_reduce_fusion
  10.7 0.1 select_reduce_fusion
  10.8 0.1 copy.46
  10.9 0.1 copy.45
  11.0 0.2 stack.11
  11.2 0.7 copy-done.5
  11.9 0.3 fusion.2
  12.1 0.3 copy.42
  12.4 0.1 pad_maximum_fusion.1
  12.5 0.1 reduce
  12.7 0.3 pad_maximum_fusion.cols_ref
  13.1 0.7 copy-done.1
  13.7 0.2 copy-done.2
  13.9 0.2 copy-done.3
  14.1 0.2 copy-done.4
  14.2 83.7 %delta_backward.1 = (bf16[128,2048]{1,0:T(8,128)(2,1)S(1)}, bf16[128,2048]{1,0:T(8,128)(2,1)S(1)}, bf16[128,2048]{1,0:T(8,128)(2,1)S(1)}, f32[8,2,128]{2,1,0:T(2,128)S(1)}, f32[8,128,2]{2,1,0:T(8,128)S(1)}) custom-call(bf16[128,2048]{1,0:T(8,128)(2,1)S(1)} %copy-done.1, bf16[128,2048]{1,0:T(8,128)(2,1)S(1)} %copy-done.2, bf16[128,2048]{1,0:T(8,128)(2,1)S(1)} %copy-done.3, ...), custom_call_target="tpu_custom_call" | custom-call | tf_op jit(solution)/shard_map/delta_backward/pallas_call | solution.py:384
  98.0 0.2 copy.48
  98.2 1.0 convolution_bitcast_fusion
  99.2 119.6 %all-reduce.3.cloned.1.call-done = f32[2304,16]{0,1:T(8,128)} async-done(((f32[2304,16]{0,1:T(8,128)}), f32[2304,16]{0,1:T(8,128)}) %all-reduce.3.cloned.1.call-update) | async-done | bytes 147472
  218.8 1.4 constant_dynamic-slice_fusion
  220.2 0.8 copy.56
  221.0 0.8 copy.57
  221.8 0.8 copy.58
  222.6 0.6 copy.59
  (21 shorter events, 0.2 us)
Async XLA Ops:
  7.2 4.0 %copy-start = (bf16[128,2304]{1,0:T(8,128)(2,1)S(1)}, bf16[128,2304]{1,0:T(8,128)(2,1)}, u32[]{:S(2)}) copy-start(bf16[128,2304]{1,0:T(8,128)(2,1)} %param.13) | copy-start | bytes 1769476
  7.2 211.6 %all-reduce.3.cloned.1.call-start = ((), (), s32[]{:S(2)}) async-start(), calls=%async_computation | async-start | bytes 294912
  8.8 0.7 copy-start.8
  8.8 0.8 copy-start.6
  9.7 0.7 copy-start.7
  11.0 0.9 copy-start.5
  12.7 1.0 copy-start.1
  12.7 1.2 copy-start.2
  12.7 1.3 copy-start.3
  12.7 1.5 copy-start.4
Sparse Core Ops, SparseCore 0:
  99.3 119.4 all-reduce.2

commit v2 on v1

--- a/solution.py
+++ b/solution.py
@@ -9,7 +9,6 @@
 
 PACK = 2
 SMALL = 16
-highest = lax.Precision.HIGHEST
 MESH = pl.DeviceIdType.MESH
 F32 = jnp.float32
 BF16 = jnp.bfloat16
@@ -91,10 +90,11 @@
 
 
 def kernel(
-    q_ref, k_ref, v_ref, o_ref, cols_ref, rows_ref,
-    dq_ref, dk_ref, dv_ref, dgate_ref, dlogit_ref,
+    q_ref, k_ref, v_ref, o_ref, cols_ref, rows_ref, hidden_ref,
+    dq_ref, dk_ref, dv_ref, dgate_ref, weight_ref,
     inv_ref, mix_ref, dkk_ref, dec_ref, map_ref, fout_ref, bout_ref, fin_ref, bin_ref,
-    fsend, frecv, bsend, brecv,
+    dlogit_ref, whole_ref, near_out, near_in, far_out, far_in,
+    fsend, frecv, bsend, brecv, nsend, nrecv, wsend, wrecv,
 ):
     tokens = q_ref.shape[0]
     groups = cols_ref.shape[0]
@@ -105,15 +105,17 @@
 
     barrier = pltpu.get_barrier_semaphore()
 
-    @pl.when(seg > 0)
-    def _():
-        pl.semaphore_signal(barrier, inc=1, device_id={"ctx": seg - 1}, device_id_type=MESH)
-
-    @pl.when(seg < last)
-    def _():
-        pl.semaphore_signal(barrier, inc=1, device_id={"ctx": seg + 1}, device_id_type=MESH)
-
-    pl.semaphore_wait(barrier, jnp.minimum(seg, 1) + jnp.minimum(last - seg, 1))
+    part = lax.axis_index("dp")
+    parts = lax.axis_size("dp")
+    for by in range(1, count):
+        pl.semaphore_signal(
+            barrier, inc=1, device_id={"ctx": lax.rem(seg + by, count)}, device_id_type=MESH
+        )
+    for by in range(1, parts):
+        pl.semaphore_signal(
+            barrier, inc=1, device_id={"dp": lax.rem(part + by, parts)}, device_id_type=MESH
+        )
+    pl.semaphore_wait(barrier, count + parts - 2)
 
     def forward_copy(group):
         return pltpu.make_async_remote_copy(
@@ -320,6 +322,53 @@
 
         return unused
 
+    logit_grad = jnp.concatenate([dlogit_ref[g] for g in range(groups)], axis=1)
+    hidden = hidden_ref[...]
+    whole_ref[...] = lax.dot_general(
+        left_t(logit_grad), stack(hidden, hidden), (((0,), (0,)), ((), ())),
+        preferred_element_type=F32,
+    )
+    owned = near_out.shape[-1]
+    for p in range(parts):
+        for c in range(count):
+            at = (p * count + c) * owned
+            near_out[p, c] = whole_ref[:, at:at + owned]
+
+    def near_copy(by):
+        to = lax.rem(part + by, parts)
+        return pltpu.make_async_remote_copy(
+            src_ref=near_out.at[to], dst_ref=near_in.at[by - 1],
+            send_sem=nsend.at[by - 1], recv_sem=nrecv.at[by - 1],
+            device_id={"dp": to}, device_id_type=MESH,
+        )
+
+    def far_copy(by):
+        to = lax.rem(seg + by, count)
+        return pltpu.make_async_remote_copy(
+            src_ref=far_out.at[to], dst_ref=far_in.at[by - 1],
+            send_sem=wsend.at[by - 1], recv_sem=wrecv.at[by - 1],
+            device_id={"ctx": to}, device_id_type=MESH,
+        )
+
+    for by in range(1, parts):
+        near_copy(by).start()
+    total = near_out[part]
+    for by in range(1, parts):
+        near_copy(by).wait_recv()
+        total = total + near_in[by - 1]
+    far_out[...] = total
+    for by in range(1, count):
+        far_copy(by).start()
+    total = far_out[seg]
+    for by in range(1, count):
+        far_copy(by).wait_recv()
+        total = total + far_in[by - 1]
+    weight_ref[...] = total
+    for by in range(1, parts):
+        near_copy(by).wait_send()
+    for by in range(1, count):
+        far_copy(by).wait_send()
+
     lax.fori_loop(0, groups, drain, 0)
 
 
@@ -381,34 +430,39 @@
     square = (groups, PACK, tokens, tokens)
     states = (groups, PACK, width, width)
     vmem = pl.BlockSpec(memory_space=pltpu.VMEM)
-    dq, dk, dv, dgate, dlogit = pl.pallas_call(
+    model = hidden_in.shape[1]
+    dp_count = lax.axis_size("dp")
+    owned = model // (dp_count * ctx_count)
+    dq, dk, dv, dgate, own_grad = pl.pallas_call(
         kernel,
         out_shape=(
             jax.ShapeDtypeStruct(queries.shape, BF16),
             jax.ShapeDtypeStruct(queries.shape, BF16),
             jax.ShapeDtypeStruct(queries.shape, BF16),
             jax.ShapeDtypeStruct((groups, PACK, tokens), F32),
-            jax.ShapeDtypeStruct((groups, tokens, PACK), F32),
+            jax.ShapeDtypeStruct((heads, owned), F32),
         ),
-        in_specs=[vmem] * 6,
+        in_specs=[vmem] * 7,
         out_specs=(vmem,) * 5,
         scratch_shapes=[pltpu.VMEM(square, F32)] * 4
         + [pltpu.VMEM(states, F32)] * 5
-        + [pltpu.SemaphoreType.DMA((groups,))] * 4,
+        + [
+            pltpu.VMEM((groups, tokens, PACK), F32),
+            pltpu.VMEM((heads, model), F32),
+            pltpu.VMEM((dp_count, ctx_count, heads, owned), F32),
+            pltpu.VMEM((dp_count - 1 or 1, ctx_count, heads, owned), F32),
+            pltpu.VMEM((ctx_count, heads, owned), F32),
+            pltpu.VMEM((ctx_count - 1, heads, owned), F32),
+        ]
+        + [pltpu.SemaphoreType.DMA((groups,))] * 4
+        + [pltpu.SemaphoreType.DMA((dp_count,))] * 2
+        + [pltpu.SemaphoreType.DMA((ctx_count,))] * 2,
         compiler_params=pltpu.CompilerParams(
             collective_id=0, has_side_effects=True, vmem_limit_bytes=48 * 2**20
         ),
         name="delta_backward",
-    )(queries, key_rows, value_rows, out_grad, columns, lines)
-    logit_grad = dlogit.transpose(1, 0, 2).reshape(tokens, heads)
-    piece = hidden_in.astype(jnp.float32)
-    beta_weight_grad = lax.psum_scatter(
-        jnp.dot(piece.T, logit_grad, precision=highest, preferred_element_type=jnp.float32),
-        ("dp", "ctx"),
-        scatter_dimension=0,
-        tiled=True,
-    )
-    return (dq, dk, dv, dgate.reshape(heads, tokens), beta_weight_grad)
+    )(queries, key_rows, value_rows, out_grad, columns, lines, hidden_in)
+    return (dq, dk, dv, dgate.reshape(heads, tokens), own_grad.T)
 
 
 def solution(mesh):

time: 232 us -> 103 us (0.44)
  waiting for transfers between devices: 120 us -> 0 us
  between operations: 14.2 us -> 0.82 us
  Pallas kernels: 83.7 us -> 92.1 us
  local copies, waits for them, and re-layouts: 9.23 us -> 6.77 us
    unnamed x2 -> x0, waiting for transfers between devices: 120 us -> none
    pallas_call x1, Pallas kernels: 83.7 us -> 92.1 us  [local(): pl.pallas_call(kernel, out_shape=(jax.ShapeDtypeStruct(queries.shape, BF1...]
    unnamed x23 -> x25, local copies, waits for them, and re-layouts: 7.52 us -> 6.05 us
  transfers between devices with their start and end apart: 1 -> 0, of which waited for: 1 -> 0; matrix products, arithmetic and copies ran while one was open for 0% -> 0% of each run, Pallas kernels for 0% -> 0%
where the time goes in v2:
time: 103 us
  Pallas kernels  92.1 us (89%)
  local copies, waits for them, and re-layouts  6.77 us (7%)
  other arithmetic  1.93 us (2%)
  matrix products  1.33 us (1%)
    pallas_call x1, Pallas kernels, local(): pl.pallas_call(kernel, out_shape=(jax.ShapeDtypeStruct(queries.shape, BF1...  92.1 us
    unnamed x25, local copies, waits for them, and re-layouts  6.05 us

profile of v2, /device:TPU:0, one launch (start us, length us, event | category | flops | bytes accessed | tf_op | source)
XLA Modules:
  0.0 103.0 jit_solution(174835280007080668)
XLA Ops:
  0.6 0.0 copy-start
  0.7 0.0 copy-start.9
  0.7 0.7 copy-done.9
  1.4 0.2 reduce-window.6
  1.5 0.1 compare_reduce_fusion
  1.6 0.6 copy-done.7
  2.3 0.0 copy-done.8
  2.3 0.2 fusion.4
  2.5 0.1 bitcast_divide_fusion
  2.6 0.1 select_reduce_fusion
  2.7 1.3 %fusion.2 = f32[128,16]{0,1:T(8,128)S(1)} fusion(bf16[128,2304]{1,0:T(8,128)(2,1)} %hidden_ref.1, bf16[2304,16]{0,1:T(8,128)(2,1)S(1)} %copy-done), kind=kOutput, calls=%fused_computation.3 | convolution fusion | flops 9443328 | bytes 671744 | tf_op jit(solution)/shard_map/dot_general | solution.py:408
  4.0 0.0 copy-done.6
  4.1 0.6 reduce_window_sum.28
  4.7 0.1 copy.43
  4.8 0.1 copy.42
  4.9 0.2 stack.11
  5.0 0.1 pad_maximum_fusion.1
  5.1 0.1 reduce
  5.3 0.2 copy.41
  5.6 0.2 copy.39
  5.8 0.3 pad_maximum_fusion.cols_ref
  6.2 0.2 copy-done.5
  6.4 0.3 copy-done.4
  6.6 0.3 copy-done.1
  7.0 0.2 copy-done.2
  7.1 0.2 copy-done.3
  7.3 92.1 %delta_backward.1 = (bf16[128,2048]{1,0:T(8,128)(2,1)S(1)}, bf16[128,2048]{1,0:T(8,128)(2,1)S(1)}, bf16[128,2048]{1,0:T(8,128)(2,1)S(1)}, f32[8,2,128]{2,1,0:T(2,128)S(1)}, f32[16,72]{1,0:T(8,128)S(1)}) custom-call(bf16[128,2048]{1,0:T(8,128)(2,1)S(1)} %copy-done.2, bf16[128,2048]{1,0:T(8,128)(2,1)S(1)} %copy-done.3, bf16[128,2048]{1,0:T(8,128)(2,1)S(1)} %copy-done.4, ...), custom_call_target="tpu_custom_call" | custom-call | tf_op jit(solution)/shard_map/delta_backward/pallas_call | solution.py:436
  99.4 0.8 copy.50
  100.2 0.8 copy.51
  101.0 0.8 copy.52
  101.8 0.6 copy.53
  102.4 0.6 copy.54
  (18 shorter events, 0.1 us)
Async XLA Ops:
  0.6 2.0 %copy-start = (bf16[2304,16]{0,1:T(8,128)(2,1)S(1)}, bf16[2304,16]{0,1:T(8,128)(2,1)}, u32[]{:S(2)}) copy-start(bf16[2304,16]{0,1:T(8,128)(2,1)} %param.14) | copy-start | bytes 221188
  0.7 0.7 copy-start.9
  1.6 0.7 copy-start.7
  1.6 0.7 copy-start.8
  2.7 1.4 %copy-start.6 = (f32[16,128]{1,0:T(8,128)S(1)}, f32[16,128]{1,0:T(8,128)}, u32[]{:S(2)}) copy-start(f32[16,128]{1,0:T(8,128)} %param.15) | copy-start | bytes 24580
  5.3 1.0 %copy-start.5 = (bf16[128,2048]{1,0:T(8,128)(2,1)S(1)}, bf16[128,2048]{1,0:T(8,128)(2,1)}, u32[]{:S(2)}) copy-start(bf16[128,2048]{1,0:T(8,128)(2,1)} %o_ref.1) | copy-start | bytes 1572868
  5.6 1.1 %copy-start.4 = (bf16[128,2048]{1,0:T(8,128)(2,1)S(1)}, bf16[128,2048]{1,0:T(8,128)(2,1)}, u32[]{:S(2)}) copy-start(bf16[128,2048]{1,0:T(8,128)(2,1)} %v_ref.1) | copy-start | bytes 1572868
  5.8 1.1 %copy-start.1 = (bf16[128,2304]{1,0:T(8,128)(2,1)S(1)}, bf16[128,2304]{1,0:T(8,128)(2,1)}, u32[]{:S(2)}) copy-start(bf16[128,2304]{1,0:T(8,128)(2,1)} %hidden_ref.1) | copy-start | bytes 1769476
  5.8 1.3 %copy-start.2 = (bf16[128,2048]{1,0:T(8,128)(2,1)S(1)}, bf16[128,2048]{1,0:T(8,128)(2,1)}, u32[]{:S(2)}) copy-start(bf16[128,2048]{1,0:T(8,128)(2,1)} %q_ref.1) | copy-start | bytes 1572868
  5.8 1.4 %copy-start.3 = (bf16[128,2048]{1,0:T(8,128)(2,1)S(1)}, bf16[128,2048]{1,0:T(8,128)(2,1)}, u32[]{:S(2)}) copy-start(bf16[128,2048]{1,0:T(8,128)(2,1)} %k_ref.1) | copy-start | bytes 1572868

commit v3 on v2

--- a/solution.py
+++ b/solution.py
@@ -8,6 +8,7 @@
 from jax.sharding import PartitionSpec as P
 
 PACK = 2
+JOIN = 2
 SMALL = 16
 MESH = pl.DeviceIdType.MESH
 F32 = jnp.float32
@@ -134,6 +135,7 @@
     rows = lax.broadcasted_iota(jnp.int32, (tokens, tokens), 0)
     cols = lax.broadcasted_iota(jnp.int32, (tokens, tokens), 1)
     heads = range(PACK)
+    batch = range(PACK * JOIN)
 
     def lanes(group, i):
         return pl.ds(pl.multiple_of((group * PACK + i) * width, width), width)
@@ -142,8 +144,9 @@
         return ref[:, lanes(group, i)].astype(F32)
 
     def token_columns(group, i):
-        block = cols_ref[group]
-        row_block = rows_ref[group]
+        block = cols_ref[group + i // PACK]
+        row_block = rows_ref[group + i // PACK]
+        i = i % PACK
         beta = block[:, i:i + 1]
         gamma = block[:, PACK + i:PACK + i + 1]
         number = block[:, 2 * PACK:2 * PACK + 1]
@@ -162,7 +165,7 @@
 
     def local_part(group):
         lows, keep = [], []
-        for i in heads:
+        for i in batch:
             beta, gamma, number, weight, gamma_row, number_row, head, tail = token_columns(group, i)
             q, k = load(q_ref, group, i), load(k_ref, group, i)
             qh, kh = q * scales(q), k * scales(k)
@@ -171,28 +174,28 @@
             both = mul_t(stack(kh, qh), kh)
             dkk = jnp.where(rows > cols, decay * both[:tokens], 0.0)
             mix = decay * both[tokens:]
-            dec_ref[group, i] = decay
-            dkk_ref[group, i] = dkk
-            mix_ref[group, i] = mix
+            dec_ref[group + i // PACK, i % PACK] = decay
+            dkk_ref[group + i // PACK, i % PACK] = dkk
+            mix_ref[group + i // PACK, i % PACK] = mix
             lows.append(beta * dkk)
             keep.append((beta, weight, head, tail, qh, kh, mix))
         invs = inverses(lows, rows, cols)
-        for i in heads:
-            inv_ref[group, i] = invs[i]
+        for i in batch:
+            inv_ref[group + i // PACK, i % PACK] = invs[i]
         pairs = []
-        for i in heads:
+        for i in batch:
             beta, weight, head, tail, qh, kh, mix = keep[i]
             v = load(v_ref, group, i)
             pairs.append(mul(invs[i], jnp.concatenate([beta * v, (beta * head) * kh], axis=1)))
         eye = jnp.where(rows == cols, 1.0, 0.0)
-        for i in heads:
+        for i in batch:
             beta, weight, head, tail, qh, kh, mix = keep[i]
             z = pairs[i][:, width:]
             ends = t_mul(pairs[i], tail * kh)
-            fout_ref[group, i] = ends[:width]
-            map_ref[group, i] = head[tokens - 1:tokens, :] * eye - ends[width:]
+            fout_ref[group + i // PACK, i % PACK] = ends[:width]
+            map_ref[group + i // PACK, i % PACK] = head[tokens - 1:tokens, :] * eye - ends[width:]
             carry = head * qh - mul(mix, z)
-            bout_ref[group, i] = t_mul(load(o_ref, group, i) * weight, carry)
+            bout_ref[group + i // PACK, i % PACK] = t_mul(load(o_ref, group, i) * weight, carry)
 
     def forward_hop(group):
         @pl.when(seg == 0)
@@ -234,28 +237,28 @@
         upper = jnp.where(rows < cols, 1.0, 0.0).astype(BF16)
         upper = stack(upper, upper)
         keep = []
-        for i in heads:
+        for i in batch:
             beta, gamma, number, weight, gamma_row, number_row, head, tail = token_columns(group, i)
             q, k = load(q_ref, group, i), load(k_ref, group, i)
             qs, ks = scales(q), scales(k)
             qh, kh = q * qs, k * ks
-            state = fin_ref[group, i]
+            state = fin_ref[group + i // PACK, i % PACK]
             both = mul_t(stack(qh, kh), state)
             keep.append((beta, weight, head, tail, qs, ks, qh, kh, state, both[:tokens], both[tokens:]))
-        rests = [load(v_ref, group, i) - keep[i][2] * keep[i][10] for i in heads]
-        us = [mul(inv_ref[group, i], keep[i][0] * rests[i]) for i in heads]
-        dos = [load(o_ref, group, i) * keep[i][1] for i in heads]
+        rests = [load(v_ref, group, i) - keep[i][2] * keep[i][10] for i in batch]
+        us = [mul(inv_ref[group + i // PACK, i % PACK], keep[i][0] * rests[i]) for i in batch]
+        dos = [load(o_ref, group, i) * keep[i][1] for i in batch]
         dus = [
-            t_mul(mix_ref[group, i], dos[i]) + mul_t(keep[i][3] * keep[i][7], bin_ref[group, i])
-            for i in heads
+            t_mul(mix_ref[group + i // PACK, i % PACK], dos[i]) + mul_t(keep[i][3] * keep[i][7], bin_ref[group + i // PACK, i % PACK])
+            for i in batch
         ]
-        drs = [t_mul(inv_ref[group, i], dus[i]) for i in heads]
-        squares = [mul_t(stack(dos[i], drs[i]), us[i]) for i in heads]
+        drs = [t_mul(inv_ref[group + i // PACK, i % PACK], dus[i]) for i in batch]
+        squares = [mul_t(stack(dos[i], drs[i]), us[i]) for i in batch]
         logit_columns = []
-        for i in heads:
+        for i in batch:
             beta, weight, head, tail, qs, ks, qh, kh, state, qstate, kstate = keep[i]
-            u, do, dr, rest, after = us[i], dos[i], drs[i], rests[i], bin_ref[group, i]
-            decay, dkk = dec_ref[group, i], dkk_ref[group, i]
+            u, do, dr, rest, after = us[i], dos[i], drs[i], rests[i], bin_ref[group + i // PACK, i % PACK]
+            decay, dkk = dec_ref[group + i // PACK, i % PACK], dkk_ref[group + i // PACK, i % PACK]
             dmix = squares[i][:tokens]
             dlow = jnp.where(rows > cols, -squares[i][tokens:], 0.0)
             inward = mul(stack(head * do, (-beta * head) * dr), state)
@@ -271,7 +274,7 @@
             dk_ref[:, lanes(group, i)] = (ks * (dkh - kh * row_sum(kh * dkh))).astype(BF16)
             dv_ref[:, lanes(group, i)] = (beta * dr).astype(BF16)
             lowpart = dlow * dkk
-            spread = dmix * mix_ref[group, i] + beta * lowpart
+            spread = dmix * mix_ref[group + i // PACK, i % PACK] + beta * lowpart
             across = lax.dot_general(
                 left(spread), upper, (((1,), (0,)), ((), ())), preferred_element_type=F32
             )
@@ -279,15 +282,18 @@
             headgrad = row_sum(do * qstate) - beta * row_sum(dr * kstate)
             headgrad = head * (headgrad + jnp.where(rows[:, :1] == tokens - 1, total, 0.0))
             tailgrad = tail * row_sum(kh * uafter)
-            dgate_ref[group, i:i + 1, :] = jnp.sum(
+            dgate_ref[group + i // PACK, i % PACK:i % PACK + 1, :] = jnp.sum(
                 jnp.where(rows >= cols, across + headgrad, tailgrad), axis=0, keepdims=True
             )
             dbeta = row_sum(dr * rest) + row_sum(lowpart)
             logit_columns.append(dbeta * beta * (1.0 - beta))
-        dlogit_ref[group] = jnp.concatenate(logit_columns, axis=1)
+        for j in range(JOIN):
+            dlogit_ref[group + j] = jnp.concatenate(
+                logit_columns[j * PACK:(j + 1) * PACK], axis=1
+            )
 
     def step(t, unused):
-        @pl.when(t < groups)
+        @pl.when((t < groups) & (lax.rem(t, JOIN) == 0))
         def _():
             local_part(t)
 
@@ -303,9 +309,11 @@
         def _():
             backward_hop(b)
 
-        @pl.when(t >= last)
-        def _():
-            gradient_part(t - last)
+        done = t - last + 1
+
+        @pl.when((done > 0) & (lax.rem(done, JOIN) == 0))
+        def _():
+            gradient_part(done - JOIN)
 
         return unused
 

time: 103 us -> 110 us (1.068)
  Pallas kernels: 92.1 us -> 98.6 us
    pallas_call x1, Pallas kernels: 92.1 us -> 98.6 us  [local(): pl.pallas_call(kernel, out_shape=(jax.ShapeDtypeStruct(queries.shape, BF1...]
where the time goes in v3:
time: 110 us; the launch traced here: 109 us
  Pallas kernels  98.6 us (90%)
  local copies, waits for them, and re-layouts  6.77 us (6%)
  other arithmetic  1.93 us (2%)
  matrix products  1.33 us (1%)
    pallas_call x1, Pallas kernels, local(): pl.pallas_call(kernel, out_shape=(jax.ShapeDtypeStruct(queries.shape, BF1...  98.6 us
    unnamed x25, local copies, waits for them, and re-layouts  6.05 us

profile of v3, /device:TPU:0, one launch (start us, length us, event | category | flops | bytes accessed | tf_op | source)
XLA Modules:
  0.0 109.4 jit_solution(13046008387574272997)
XLA Ops:
  0.6 0.0 copy-start
  0.7 0.7 copy-done.9
  1.4 0.2 reduce-window.6
  1.5 0.1 compare_reduce_fusion
  1.6 0.6 copy-done.7
  2.3 0.0 copy-done.8
  2.3 0.2 fusion.4
  2.5 0.1 bitcast_divide_fusion
  2.6 0.1 select_reduce_fusion
  2.7 1.3 %fusion.2 = f32[128,16]{0,1:T(8,128)S(1)} fusion(bf16[128,2304]{1,0:T(8,128)(2,1)} %hidden_ref.1, bf16[2304,16]{0,1:T(8,128)(2,1)S(1)} %copy-done), kind=kOutput, calls=%fused_computation.3 | convolution fusion | flops 9443328 | bytes 671744 | tf_op jit(solution)/shard_map/dot_general | solution.py:416
  4.0 0.0 copy-done.6
  4.1 0.6 reduce_window_sum.28
  4.7 0.1 copy.43
  4.8 0.1 copy.42
  4.9 0.2 stack.11
  5.0 0.1 pad_maximum_fusion.1
  5.1 0.1 reduce
  5.3 0.2 copy.41
  5.6 0.2 copy.39
  5.8 0.0 copy-start.1
  5.8 0.3 pad_maximum_fusion.cols_ref
  6.2 0.2 copy-done.5
  6.4 0.3 copy-done.4
  6.6 0.3 copy-done.1
  7.0 0.2 copy-done.2
  7.1 0.2 copy-done.3
  7.3 98.6 %delta_backward.1 = (bf16[128,2048]{1,0:T(8,128)(2,1)S(1)}, bf16[128,2048]{1,0:T(8,128)(2,1)S(1)}, bf16[128,2048]{1,0:T(8,128)(2,1)S(1)}, f32[8,2,128]{2,1,0:T(2,128)S(1)}, f32[16,72]{1,0:T(8,128)S(1)}) custom-call(bf16[128,2048]{1,0:T(8,128)(2,1)S(1)} %copy-done.2, bf16[128,2048]{1,0:T(8,128)(2,1)S(1)} %copy-done.3, bf16[128,2048]{1,0:T(8,128)(2,1)S(1)} %copy-done.4, ...), custom_call_target="tpu_custom_call" | custom-call | tf_op jit(solution)/shard_map/delta_backward/pallas_call | solution.py:444
  105.8 0.8 copy.50
  106.6 0.8 copy.51
  107.4 0.8 copy.52
  108.2 0.6 copy.53
  108.8 0.6 copy.54
  (18 shorter events, 0.1 us)
Async XLA Ops:
  0.6 2.0 %copy-start = (bf16[2304,16]{0,1:T(8,128)(2,1)S(1)}, bf16[2304,16]{0,1:T(8,128)(2,1)}, u32[]{:S(2)}) copy-start(bf16[2304,16]{0,1:T(8,128)(2,1)} %param.14) | copy-start | bytes 221188
  0.7 0.7 copy-start.9
  1.6 0.7 copy-start.7
  1.6 0.7 copy-start.8
  2.7 1.4 %copy-start.6 = (f32[16,128]{1,0:T(8,128)S(1)}, f32[16,128]{1,0:T(8,128)}, u32[]{:S(2)}) copy-start(f32[16,128]{1,0:T(8,128)} %param.15) | copy-start | bytes 24580
  5.3 1.0 copy-start.5
  5.6 1.1 copy-start.4
  5.8 1.1 %copy-start.1 = (bf16[128,2304]{1,0:T(8,128)(2,1)S(1)}, bf16[128,2304]{1,0:T(8,128)(2,1)}, u32[]{:S(2)}) copy-start(bf16[128,2304]{1,0:T(8,128)(2,1)} %hidden_ref.1) | copy-start | bytes 1769476
  5.8 1.3 %copy-start.2 = (bf16[128,2048]{1,0:T(8,128)(2,1)S(1)}, bf16[128,2048]{1,0:T(8,128)(2,1)}, u32[]{:S(2)}) copy-start(bf16[128,2048]{1,0:T(8,128)(2,1)} %q_ref.1) | copy-start | bytes 1572868
  5.8 1.4 %copy-start.3 = (bf16[128,2048]{1,0:T(8,128)(2,1)S(1)}, bf16[128,2048]{1,0:T(8,128)(2,1)}, u32[]{:S(2)}) copy-start(bf16[128,2048]{1,0:T(8,128)(2,1)} %k_ref.1) | copy-start | bytes 1572868
